TPU v7x, 32 devices: a whole 2x2x4 slice. The times are simulated.
32 devices in a mesh: rep: 4 (over y, x), shard: 8 (over z, core).
Axes of the slice: x: 2, y: 2, z: 4, core: 2. Of those that a mesh axis runs over, the one named last changes fastest.
Arguments:
- tokens: bfloat16 [8192, 2048], P(('rep', 'shard')), may hold values from -6 to 6
- lengths: int32 [32], P(('rep', 'shard')), may hold values from 128 to 256, as said below
- routes: int32 [8192, 8], P(('rep', 'shard')), may hold values from 0 to 15, all different within a row; in each aligned block of 256 rows (0 to 255, 256 to 511, ...) at most 144 rows name the same one
- gain_attn: float32 [2048], replicated, may hold values from 0.1 to 1.9
- gain_query: float32 [128], replicated, may hold values from 0.1 to 1.9
- gain_key: float32 [128], replicated, may hold values from 0.1 to 1.9
- w_query: bfloat16 [2048, 2048], P(None, 'shard'), may hold values from -0.125 to 0.125
- w_key: bfloat16 [2048, 2048], P(None, 'shard'), may hold values from -0.125 to 0.125
- w_value: bfloat16 [2048, 2048], P(None, 'shard'), may hold values from -0.125 to 0.125
- w_out: bfloat16 [2048, 2048], P('shard'), may hold values from -0.75 to 0.75
- gain_moe: float32 [2048], replicated, may hold values from 0.1 to 1.9
- w_router: bfloat16 [2048, 16], replicated, may hold values from -0.0625 to 0.0625
- w_gate: bfloat16 [16, 2048, 1024], P('shard'), may hold values from -0.125 to 0.125
- w_up: bfloat16 [16, 2048, 1024], P('shard'), may hold values from -0.125 to 0.125
- w_down: bfloat16 [16, 1024, 2048], P('shard'), may hold values from -1.5 to 1.5
- out_grad: bfloat16 [8192, 2048], P(('rep', 'shard')), may hold values from -6 to 6
Outputs:
- output: bfloat16 [8192, 2048], P(('rep', 'shard'))
- input_grad: float32 [8192, 2048], P(('rep', 'shard'))
- grad_gain_attn: float32 [2048], replicated
- grad_gain_query: float32 [128], replicated
- grad_gain_key: float32 [128], replicated
- grad_w_query: float32 [2048, 2048], P(None, 'shard')
- grad_w_key: float32 [2048, 2048], P(None, 'shard')
- grad_w_value: float32 [2048, 2048], P(None, 'shard')
- grad_w_out: float32 [2048, 2048], P('shard')
- grad_gain_moe: float32 [2048], replicated
- grad_w_router: float32 [2048, 16], replicated
- grad_w_gate: float32 [16, 2048, 1024], P('shard')
- grad_w_up: float32 [16, 2048, 1024], P('shard')
- grad_w_down: float32 [16, 1024, 2048], P('shard')
Inputs may be any that keep to these rules, and one draw needn't show every extreme that they name: `lengths`: valid tokens of each sequence; some sequence is full. `routes`: each row names 8 different experts; among the 256 rows of one sequence no expert is named by more than 144 rows, a bound that some block reaches.
All inputs are finite; a program needn't handle non-finite values.
Results may differ from a plain program's by a relative error of at most 0.024.
Values may be sent and summed in bfloat16 or wider, within the bound.
A program may use at most 320 MiB of HBM per device.

v0:
```python
import jax
import jax.numpy as jnp
from jax import lax
from jax.sharding import PartitionSpec as P

CAP = 144
EPS_NORM = 1e-06
ROPE_BASE = 50000.0
MASKED = -1e30


def rms_scale(values, gain_vec):
    return (
        values * lax.rsqrt(jnp.mean(values * values, axis=-1, keepdims=True) + EPS_NORM) * gain_vec
    )


def rope_tables(seq_len, head_dim):
    half_dim = head_dim // 2
    places = jnp.arange(seq_len, dtype=jnp.float32)
    freqs = ROPE_BASE ** (-jnp.arange(half_dim, dtype=jnp.float32) * (2.0 / head_dim))
    angles = places[:, None] * freqs[None, :]
    cos_tab = jnp.concatenate([jnp.cos(angles), jnp.cos(angles)], axis=-1)
    sine_tab = jnp.concatenate([jnp.sin(angles), jnp.sin(angles)], axis=-1)
    return (cos_tab, sine_tab)


def rotate_half(values, cos_tab, sine_tab):
    half_dim = values.shape[-1] // 2
    turned = jnp.concatenate([-values[..., half_dim:], values[..., :half_dim]], axis=-1)
    return values * cos_tab[:, None, :] + turned * sine_tab[:, None, :]


def head_prepare(raw_proj, gain_vec, cos_tab, sine_tab):
    return rotate_half(rms_scale(raw_proj, gain_vec), cos_tab, sine_tab)


def soft_max(logit_vals):
    upper = jnp.max(logit_vals, axis=-1, keepdims=True)
    expo = jnp.exp(logit_vals - upper)
    return expo / jnp.sum(expo, axis=-1, keepdims=True)


def slot_table(route_rows, expert_count):
    flat_ids = route_rows.reshape(-1)
    one_hot = (flat_ids[:, None] == jnp.arange(expert_count, dtype=jnp.int32)[None, :]).astype(
        jnp.int32
    )
    before = jnp.cumsum(one_hot, axis=0) - one_hot
    ranks = jnp.sum(before * one_hot, axis=1)
    return flat_ids * CAP + ranks


def attend(query_rot, key_rot, value_low, key_valid, score_scale):
    scores = (
        jnp.einsum("sqhd,skhd->shqk", query_rot, key_rot, preferred_element_type=jnp.float32)
        * score_scale
    )
    scores = jnp.where(key_valid[:, None, None, :], scores, MASKED)
    upper = jnp.max(scores, axis=-1, keepdims=True)
    expo = jnp.exp(scores - upper)
    total = jnp.sum(expo, axis=-1, keepdims=True)
    weights = (expo / total).astype(jnp.bfloat16)
    result = jnp.einsum("shqk,skhd->sqhd", weights, value_low, preferred_element_type=jnp.float32)
    return (result.astype(jnp.bfloat16), upper + jnp.log(total))


def attend_back(query_rot, key_rot, value_low, key_valid, score_scale, log_total, grad_result):
    scores = (
        jnp.einsum("sqhd,skhd->shqk", query_rot, key_rot, preferred_element_type=jnp.float32)
        * score_scale
    )
    scores = jnp.where(key_valid[:, None, None, :], scores, MASKED)
    probs_full = jnp.exp(scores - log_total)
    weights = probs_full.astype(jnp.bfloat16)
    grad_value = jnp.einsum(
        "shqk,sqhd->skhd", weights, grad_result, preferred_element_type=jnp.float32
    ).astype(jnp.bfloat16)
    grad_prob = jnp.einsum(
        "sqhd,skhd->shqk", grad_result, value_low, preferred_element_type=jnp.float32
    )
    mean_term = jnp.sum(probs_full * grad_prob, axis=-1, keepdims=True)
    grad_score = (probs_full * (grad_prob - mean_term)).astype(jnp.bfloat16)
    grad_query = (
        jnp.einsum("shqk,skhd->sqhd", grad_score, key_rot, preferred_element_type=jnp.float32)
        * score_scale
    )
    grad_key = (
        jnp.einsum("shqk,sqhd->skhd", grad_score, query_rot, preferred_element_type=jnp.float32)
        * score_scale
    )
    return (grad_query, grad_key, grad_value)


def local(
    tokens,
    lengths,
    routes,
    gain_attn,
    gain_query,
    gain_key,
    w_query,
    w_key,
    w_value,
    w_out,
    gain_moe,
    w_router,
    w_gate,
    w_up,
    w_down,
    out_grad,
):
    row_count, model_width = tokens.shape
    head_dim = gain_query.shape[0]
    group_count = lax.axis_size("shard")
    expert_count = w_router.shape[1]
    inputs = tokens.astype(jnp.float32)
    row_valid = jnp.arange(row_count, dtype=jnp.int32) < lengths[0]
    row_mask = row_valid.astype(jnp.float32)
    cos_tab, sine_tab = rope_tables(row_count, head_dim)
    score_scale = head_dim ** (-0.5)
    normed_low = rms_scale(inputs, gain_attn).astype(jnp.bfloat16)
    source, key_marks = (
        lax.all_gather(normed_low, "shard", axis=0, tiled=True),
        lax.all_gather(row_mask.astype(jnp.bfloat16), "shard", axis=0, tiled=True),
    )
    key_valid = key_marks.reshape(group_count, row_count) > 0.5
    proj_query, proj_key, proj_value, proj_out = (w_query, w_key, w_value, w_out)
    head_local = proj_query.shape[1] // head_dim
    four_shape = (group_count, row_count, head_local, head_dim)
    flat_shape = (group_count * row_count, head_local * head_dim)
    query_raw = jnp.dot(source, proj_query, preferred_element_type=jnp.float32).reshape(four_shape)
    key_raw = jnp.dot(source, proj_key, preferred_element_type=jnp.float32).reshape(four_shape)
    value_low = jnp.dot(source, proj_value, preferred_element_type=jnp.float32).astype(jnp.bfloat16)
    value_low = value_low.reshape(four_shape)
    query_rot = head_prepare(query_raw, gain_query, cos_tab, sine_tab).astype(jnp.bfloat16)
    key_rot = head_prepare(key_raw, gain_key, cos_tab, sine_tab).astype(jnp.bfloat16)
    attended, log_total = attend(query_rot, key_rot, value_low, key_valid, score_scale)
    flat_attended = attended.reshape(flat_shape)
    branch = lax.psum_scatter(
        jnp.dot(flat_attended, proj_out, preferred_element_type=jnp.float32),
        "shard",
        scatter_dimension=0,
        tiled=True,
    )
    hidden = inputs + branch
    moe_low = rms_scale(hidden, gain_moe).astype(jnp.bfloat16)
    router_probs = soft_max(jnp.dot(moe_low, w_router, preferred_element_type=jnp.float32))
    route_hot = (
        routes[:, :, None] == jnp.arange(expert_count, dtype=jnp.int32)[None, None, :]
    ).astype(jnp.float32)
    gate_vals = jnp.sum(router_probs[:, None, :] * route_hot, axis=-1)
    slot_ids = slot_table(routes, expert_count)
    copies = jnp.repeat(moe_low, routes.shape[1], axis=0)
    send_rows = jnp.zeros((expert_count * CAP, model_width), jnp.bfloat16).at[slot_ids].set(copies)
    arrived = lax.all_to_all(
        send_rows.reshape(expert_count, CAP, model_width),
        "shard",
        split_axis=0,
        concat_axis=1,
        tiled=True,
    )
    gate_act = jnp.einsum("erd,edf->erf", arrived, w_gate, preferred_element_type=jnp.float32)
    up_act = jnp.einsum("erd,edf->erf", arrived, w_up, preferred_element_type=jnp.float32)
    sig_gate = jax.nn.sigmoid(gate_act)
    silu_gate = gate_act * sig_gate
    joined = (silu_gate * up_act).astype(jnp.bfloat16)
    expert_out = jnp.einsum(
        "erf,efd->erd", joined, w_down, preferred_element_type=jnp.float32
    ).astype(jnp.bfloat16)
    returned = lax.all_to_all(expert_out, "shard", split_axis=1, concat_axis=0, tiled=True).reshape(
        expert_count * CAP, model_width
    )
    picked = returned[slot_ids].astype(jnp.float32).reshape(row_count, -1, model_width)
    mixture = jnp.sum(picked * gate_vals[:, :, None], axis=1)
    output = (hidden + mixture).astype(jnp.bfloat16)
    grad_out = out_grad.astype(jnp.float32) * row_mask[:, None]
    grad_gates = jnp.sum(picked * grad_out[:, None, :], axis=-1)
    grad_rows = (
        (gate_vals[:, :, None] * grad_out[:, None, :]).astype(jnp.bfloat16).reshape(-1, model_width)
    )
    grad_send = (
        jnp.zeros((expert_count * CAP, model_width), jnp.bfloat16).at[slot_ids].set(grad_rows)
    )
    grad_arrived = lax.all_to_all(
        grad_send.reshape(expert_count, CAP, model_width),
        "shard",
        split_axis=0,
        concat_axis=1,
        tiled=True,
    )
    grad_joined = jnp.einsum(
        "erd,efd->erf", grad_arrived, w_down, preferred_element_type=jnp.float32
    )
    grad_down = jnp.einsum("erf,erd->efd", joined, grad_arrived, preferred_element_type=jnp.float32)
    grad_gate_act = (grad_joined * up_act * sig_gate * (1.0 + gate_act * (1.0 - sig_gate))).astype(
        jnp.bfloat16
    )
    grad_up_act = (grad_joined * silu_gate).astype(jnp.bfloat16)
    grad_expert_in = jnp.einsum(
        "erf,edf->erd", grad_gate_act, w_gate, preferred_element_type=jnp.float32
    ) + jnp.einsum("erf,edf->erd", grad_up_act, w_up, preferred_element_type=jnp.float32)
    grad_expert_in = grad_expert_in.astype(jnp.bfloat16)
    grad_gate_w = jnp.einsum(
        "erd,erf->edf", arrived, grad_gate_act, preferred_element_type=jnp.float32
    )
    grad_up_w = jnp.einsum("erd,erf->edf", arrived, grad_up_act, preferred_element_type=jnp.float32)
    grad_back = lax.all_to_all(
        grad_expert_in, "shard", split_axis=1, concat_axis=0, tiled=True
    ).reshape(expert_count * CAP, model_width)
    grad_moe_in = jnp.sum(
        grad_back[slot_ids].astype(jnp.float32).reshape(row_count, -1, model_width), axis=1
    )
    grad_probs = jnp.sum(grad_gates[:, :, None] * route_hot, axis=1)
    grad_logits = router_probs * (
        grad_probs - jnp.sum(router_probs * grad_probs, axis=-1, keepdims=True)
    )
    router_full = w_router.astype(jnp.float32)
    grad_moe_in = grad_moe_in + jnp.dot(grad_logits, router_full.T, precision=lax.Precision.HIGHEST)
    grad_router = jnp.dot(
        moe_low.astype(jnp.float32).T, grad_logits, precision=lax.Precision.HIGHEST
    )
    moe_unused, pull_moe = jax.vjp(rms_scale, hidden, gain_moe)
    grad_hidden_part, grad_gain_moe = pull_moe(grad_moe_in)
    grad_hidden = grad_out + grad_hidden_part
    grad_branch = grad_hidden.astype(jnp.bfloat16)
    branch_rows = lax.all_gather(grad_branch, "shard", axis=0, tiled=True)
    grad_attended = jnp.dot(branch_rows, proj_out.T, preferred_element_type=jnp.float32).astype(
        jnp.bfloat16
    )
    grad_out_w = jnp.dot(flat_attended.T, branch_rows, preferred_element_type=jnp.float32)
    grad_query_rot, grad_key_rot, grad_value = attend_back(
        query_rot,
        key_rot,
        value_low,
        key_valid,
        score_scale,
        log_total,
        grad_attended.reshape(four_shape),
    )

    def prepare(raw_proj, gain_vec):
        return head_prepare(raw_proj, gain_vec, cos_tab, sine_tab)

    query_unused, pull_query = jax.vjp(prepare, query_raw, gain_query)
    grad_query_raw, grad_gain_query = pull_query(grad_query_rot)
    key_unused, pull_key = jax.vjp(prepare, key_raw, gain_key)
    grad_key_raw, grad_gain_key = pull_key(grad_key_rot)
    grad_q_low = grad_query_raw.astype(jnp.bfloat16).reshape(flat_shape)
    grad_k_low = grad_key_raw.astype(jnp.bfloat16).reshape(flat_shape)
    grad_v_low = grad_value.reshape(flat_shape)
    grad_query_w = jnp.dot(source.T, grad_q_low, preferred_element_type=jnp.float32)
    grad_key_w = jnp.dot(source.T, grad_k_low, preferred_element_type=jnp.float32)
    grad_value_w = jnp.dot(source.T, grad_v_low, preferred_element_type=jnp.float32)
    grad_normed = lax.psum_scatter(
        (
            jnp.dot(grad_q_low, proj_query.T, preferred_element_type=jnp.float32)
            + jnp.dot(grad_k_low, proj_key.T, preferred_element_type=jnp.float32)
            + jnp.dot(grad_v_low, proj_value.T, preferred_element_type=jnp.float32)
        ).astype(jnp.bfloat16),
        "shard",
        scatter_dimension=0,
        tiled=True,
    ).astype(jnp.float32)
    attn_unused, pull_attn = jax.vjp(rms_scale, inputs, gain_attn)
    grad_input_part, grad_gain_attn = pull_attn(grad_normed)
    grad_input = grad_hidden + grad_input_part
    summed = (
        lax.psum(grad_query_w.astype(jnp.bfloat16), "rep").astype(jnp.float32),
        lax.psum(grad_key_w.astype(jnp.bfloat16), "rep").astype(jnp.float32),
        lax.psum(grad_value_w.astype(jnp.bfloat16), "rep").astype(jnp.float32),
        lax.psum(grad_out_w.astype(jnp.bfloat16), "rep").astype(jnp.float32),
        lax.psum(grad_gate_w.astype(jnp.bfloat16), "rep").astype(jnp.float32),
        lax.psum(grad_up_w.astype(jnp.bfloat16), "rep").astype(jnp.float32),
        lax.psum(grad_down.astype(jnp.bfloat16), "rep").astype(jnp.float32),
    )
    shared = lax.psum(
        (grad_gain_attn, grad_gain_query, grad_gain_key, grad_gain_moe, grad_router),
        ("rep", "shard"),
    )
    return (
        output,
        grad_input,
        shared[0],
        shared[1],
        shared[2],
        summed[0],
        summed[1],
        summed[2],
        summed[3],
        shared[3],
        shared[4],
        summed[4],
        summed[5],
        summed[6],
    )


def solution(mesh):
    return jax.shard_map(
        local,
        mesh=mesh,
        in_specs=(
            P(("rep", "shard"), None),
            P(("rep", "shard")),
            P(("rep", "shard"), None),
            P(),
            P(),
            P(),
            P(None, "shard"),
            P(None, "shard"),
            P(None, "shard"),
            P("shard", None),
            P(),
            P(),
            P("shard", None, None),
            P("shard", None, None),
            P("shard", None, None),
            P(("rep", "shard"), None),
        ),
        out_specs=(
            P(("rep", "shard"), None),
            P(("rep", "shard"), None),
            P(),
            P(),
            P(),
            P(None, "shard"),
            P(None, "shard"),
            P(None, "shard"),
            P("shard", None),
            P(),
            P(),
            P("shard", None, None),
            P("shard", None, None),
            P("shard", None, None),
        ),
        check_vma=False,
    )
```

profile of v0, /device:TPU:0, one launch (start us, length us, event | category | flops | bytes accessed | tf_op | source)
XLA Modules:
  0.0 2252.7 jit_solution(6892973722710807610)
XLA Ops:
  28.4 69.1 %all-gather.4.cloned.1.call-done = bf16[2048,2048]{1,0:T(8,128)(2,1)} async-done(((bf16[256,2048]{1,0:T(8,128)(2,1)}), bf16[2048,2048]{1,0:T(8,128)(2,1)}) %all-gather.4.cloned.1.call-update) | async-done | bytes 8388624 | tf_op jit(solution)/shard_map/all_gather | solution.py:124
  174.2 158.8 %reduce-scatter.3.cloned.1.call-done = f32[256,2048]{1,0:T(8,128)} async-done(((f32[2048,2048]{1,0:T(8,128)}), f32[256,2048]{1,0:T(8,128)}) %reduce-scatter.3.cloned.1.call-update) | async-done | bytes 2097168 | tf_op jit(solution)/shard_map/reduce_scatter | solution.py:140
  339.4 18.5 scatter_custom_fusion.1
  363.4 17.6 scatter_custom_fusion
  381.0 188.8 %all-to-all-done.2 = bf16[16,144,2048]{2,1,0:T(8,128)(2,1)} async-done(((bf16[16,144,2048]{2,1,0:T(8,128)(2,1)}), bf16[16,144,2048]{2,1,0:T(8,128)(2,1)}, u32[]{:S(2)}, u32[]{:S(2)}) %all-to-all-start.2) | async-done | bytes 9437216 | tf_op jit(solution)/shard_map/all_to_all | solution.py:185
  584.3 197.1 %all-to-all-done = bf16[16,144,2048]{2,1,0:T(8,128)(2,1)} async-done(((bf16[16,144,2048]{2,1,0:T(8,128)(2,1)}), bf16[16,144,2048]{2,1,0:T(8,128)(2,1)}, u32[]{:S(2)}, u32[]{:S(2)}) %all-to-all-start) | async-done | bytes 9437216 | tf_op jit(solution)/shard_map/all_to_all | solution.py:156
  790.8 17.2 fusion.76
  822.5 23.1 %multiply_convert_fusion = (bf16[2,1152,1024]{2,1,0:T(8,128)(2,1)}, bf16[2,1152,1024]{2,1,0:T(8,128)(2,1)}, bf16[2,1152,1024]{2,1,0:T(8,128)(2,1)}) fusion(f32[2,1152,1024]{2,1,0:T(8,128)} %fusion.75, f32[2,1152,1024]{2,1,0:T(8,128)} %fusion.76, bf16[2,1152,2048]{2,1,0:T(8,128)(2,1)} %bitcast.161, bf16[2,1024,2048]{2,1,0:T(8,128)(2,1)} %param.30), kind=kOutput, calls=%fused_computation.14 | convolution fusion | flops 9699065856 | bytes 50855936 | tf_op jit(solution)/shard_map/erd,efd->erf/dot_general | solution.py:192
  859.9 27.9 %copy.302 = bf16[2,1152,2048]{2,0,1:T(2,128)(2,1)} copy(bf16[2,1152,2048]{2,1,0:T(8,128)(2,1)S(1)} %convolution_convert_fusion) | data formatting | bytes 18874368 | tf_op jit(solution)/shard_map/convert_element_type | solution.py:170
  893.1 17.5 fusion.77
  910.6 18.6 add_convert_fusion
  929.2 18.2 copy.307
  947.4 152.0 %all-to-all-done.1 = bf16[2,1152,2048]{2,0,1:T(2,128)(2,1)} async-done(((bf16[2,1152,2048]{2,0,1:T(2,128)(2,1)}), bf16[2,1152,2048]{2,0,1:T(2,128)(2,1)}, u32[]{:S(2)}, u32[]{:S(2)}) %all-to-all-start.1) | async-done | bytes 9437216 | tf_op jit(solution)/shard_map/all_to_all | solution.py:171
  1116.7 21.6 gather_fusion
  1148.0 162.9 %all-to-all-done.3 = bf16[2,1152,2048]{2,0,1:T(2,128)(2,1)} async-done(((bf16[2,1152,2048]{2,0,1:T(2,128)(2,1)}), bf16[2,1152,2048]{2,0,1:T(2,128)(2,1)}, u32[]{:S(2)}, u32[]{:S(2)}) %all-to-all-start.3) | async-done | bytes 9437216 | tf_op jit(solution)/shard_map/all_to_all | solution.py:208
  1322.7 21.6 gather_fusion.1
  1362.9 80.9 %all-gather.6.cloned.1.call-done = bf16[2048,2048]{1,0:T(8,128)(2,1)} async-done(((bf16[256,2048]{1,0:T(8,128)(2,1)}), bf16[2048,2048]{1,0:T(8,128)(2,1)}) %all-gather.6.cloned.1.call-update) | async-done | bytes 8388624 | tf_op jit(solution)/shard_map/all_gather | solution.py:227
  1487.5 15.6 add_convert_fusion.1
  1503.2 18.8 convolution_convert_fusion.1
  1522.0 17.2 convolution_convert_fusion.2
  1539.3 15.7 convolution_convert_fusion.3
  1597.5 38.8 %all-reduce.4 = (f32[2048]{0:T(1024)}, f32[128]{0:T(128)}, f32[128]{0:T(128)}, f32[2048]{0:T(1024)}) all-reduce(f32[2048]{0:T(1024)S(1)} %get-tuple-element.22, f32[128]{0:T(128)S(1)} %get-tuple-element.56, f32[128]{0:T(128)S(1)} %get-tuple-element.18, f32[2048]{0:T(1024)S(1)} %copy-done.65), channel_id=1, replica_groups=mesh['rep'=4,'shard'=8] {'rep','shard'}, use_global_device_ids=true, to_apply=%region_27.28 | all-reduce | flops 4352 | bytes 34816 | tf_op jit(solution)/shard_map/psum | solution.py:277
  1636.3 478.5 %all-reduce.11.cloned.1.call-done = (bf16[2048,256]{1,0:T(8,128)(2,1)}, bf16[2048,256]{1,0:T(8,128)(2,1)}, bf16[2048,256]{1,0:T(8,128)(2,1)}, bf16[256,2048]{1,0...) async-done(((bf16[2048,256]{1,0:T(8,128)(2,1)}, bf16[2048,256]{1,0:T(8,128)(2,1)}, ...) | async-done | bytes 29360144 | tf_op jit(solution)/shard_map/psum | solution.py:269
  2158.5 85.6 %all-reduce.9.cloned.1.call-done = f32[2048,16]{0,1:T(8,128)} async-done(((f32[2048,16]{0,1:T(8,128)}), f32[2048,16]{0,1:T(8,128)}) %all-reduce.9.cloned.1.call-update) | async-done | bytes 131088 | tf_op jit(solution)/shard_map/psum | solution.py:277
  (323 shorter events, 354.6 us)
Async XLA Ops:
  7.2 150.2 %copy-start = (bf16[256,2048]{1,0:T(8,128)(2,1)S(1)}, bf16[256,2048]{1,0:T(8,128)(2,1)}, u32[]{:S(2)}) copy-start(bf16[256,2048]{1,0:T(8,128)(2,1)} %param.25) | copy-start | bytes 3145732
  7.2 90.3 %copy-start.33 = (bf16[2048,256]{1,0:T(8,128)(2,1)S(1)}, bf16[2048,256]{1,0:T(8,128)(2,1)}, u32[]{:S(2)}) copy-start(bf16[2048,256]{1,0:T(8,128)(2,1)} %param.23) | copy-start | bytes 3145732
  7.2 90.3 %all-gather.4.cloned.1.call-start = ((), (), s32[]{:S(2)}) async-start(), calls=%async_computation.6 | async-start | bytes 9437184 | tf_op jit(solution)/shard_map/all_gather | solution.py:124
  12.6 320.3 %reduce-scatter.3.cloned.1.call-start = ((), (), s32[]{:S(2)}) async-start(), calls=%async_computation.7 | async-start | bytes 18874368 | tf_op jit(solution)/shard_map/reduce_scatter | solution.py:140
  114.5 33.7 %copy-start.3 = (f32[8,256,2,128]{1,3,2,0:T(8,128)}, f32[8,256,2,128]{1,3,2,0:T(8,128)S(1)}, u32[]{:S(2)}) copy-start(f32[8,256,2,128]{1,3,2,0:T(8,128)S(1)} %copy.292) | copy-start | bytes 6291460
  166.6 166.3 %copy-start.8 = (bf16[256,2048]{1,0:T(8,128)(2,1)S(1)}, bf16[256,2048]{1,0:T(8,128)(2,1)}, u32[]{:S(2)}) copy-start(bf16[256,2048]{1,0:T(8,128)(2,1)} %param.16) | copy-start | bytes 3145732
  172.4 162.5 %copy-start.86 = (f32[256]{0:T(256)}, f32[256]{0:T(256)S(1)}, u32[]{:S(2)}) copy-start(f32[256]{0:T(256)S(1)} %compare_convert_fusion) | copy-start | bytes 3076
  172.6 190.8 %copy-start.66 = (s32[2048,1]{0,1:T(1,128)}, s32[2048,1]{0,1:T(1,128)S(1)}, u32[]{:S(2)}) copy-start(s32[2048,1]{0,1:T(1,128)S(1)} %compare_select_fusion) | copy-start | bytes 24580
  172.6 163.6 %copy-start.61 = (f32[2048]{0:T(1024)S(1)}, f32[2048]{0:T(1024)}, u32[]{:S(2)}) copy-start(f32[2048]{0:T(1024)} %param.26) | copy-start | bytes 24580
  174.2 163.3 %copy-start.39 = (bf16[2048,16]{0,1:T(8,128)(2,1)S(1)}, bf16[2048,16]{0,1:T(8,128)(2,1)}, u32[]{:S(2)}) copy-start(bf16[2048,16]{0,1:T(8,128)(2,1)} %param.27) | copy-start | bytes 196612
  358.0 211.7 %all-to-all-start.2 = ((bf16[16,144,2048]{2,1,0:T(8,128)(2,1)}), bf16[16,144,2048]{2,1,0:T(8,128)(2,1)}, u32[]{:S(2)}, u32[]{:S(2)}) async-start(bf16[16,144,2048]{2,1,0:T(8,128)(2,1)} %bitcast.160), calls=%async_computation.3 | async-start | bytes 18874368 | tf_op jit(solution)/shard_map/all_to_all | solution.py:185
  569.7 211.7 %all-to-all-start = ((bf16[16,144,2048]{2,1,0:T(8,128)(2,1)}), bf16[16,144,2048]{2,1,0:T(8,128)(2,1)}, u32[]{:S(2)}, u32[]{:S(2)}) async-start(bf16[16,144,2048]{2,1,0:T(8,128)(2,1)} %bitcast.159), calls=%async_computation.1 | async-start | bytes 18874368 | tf_op jit(solution)/shard_map/all_to_all | solution.py:156
  887.8 211.7 %all-to-all-start.1 = ((bf16[2,1152,2048]{2,0,1:T(2,128)(2,1)}), bf16[2,1152,2048]{2,0,1:T(2,128)(2,1)}, u32[]{:S(2)}, u32[]{:S(2)}) async-start(bf16[2,1152,2048]{2,0,1:T(2,128)(2,1)} %copy.302), calls=%async_computation.2 | async-start | bytes 18874368 | tf_op jit(solution)/shard_map/all_to_all | solution.py:171
  947.4 157.4 %copy-start.67 = (s32[2048,1]{0,1:T(1,128)S(1)}, s32[2048,1]{0,1:T(1,128)}, u32[]{:S(2)}) copy-start(s32[2048,1]{0,1:T(1,128)} %copy-done.66) | copy-start | bytes 24580
  1099.4 211.4 %all-to-all-start.3 = ((bf16[2,1152,2048]{2,0,1:T(2,128)(2,1)}), bf16[2,1152,2048]{2,0,1:T(2,128)(2,1)}, u32[]{:S(2)}, u32[]{:S(2)}) async-start(bf16[2,1152,2048]{2,0,1:T(2,128)(2,1)} %copy.307), calls=%async_computation.4 | async-start | bytes 18874368 | tf_op jit(solution)/shard_map/all_to_all | solution.py:208
  1104.5 339.3 %all-gather.6.cloned.1.call-start = ((), (), s32[]{:S(2)}) async-start(), calls=%async_computation.8 | async-start | bytes 9437184 | tf_op jit(solution)/shard_map/all_gather | solution.py:227
  1116.7 21.7 copy-start.31
  1147.9 207.9 %copy-start.44 = (f32[256,16]{0,1:T(8,128)}, f32[256,16]{0,1:T(8,128)S(1)}, u32[]{:S(2)}) copy-start(f32[256,16]{0,1:T(8,128)S(1)} %select_reduce_fusion) | copy-start | bytes 49156
  1148.0 207.9 %copy-start.78 = (f32[256]{0:T(256)}, f32[256]{0:T(256)S(1)}, u32[]{:S(2)}) copy-start(f32[256]{0:T(256)S(1)} %multiply_reduce_fusion.10) | copy-start | bytes 3076
  1362.9 228.6 %reduce-scatter.5.cloned.1.call-start = ((), (), s32[]{:S(2)}) async-start(), calls=%async_computation.9 | async-start | bytes 9437184 | tf_op jit(solution)/shard_map/reduce_scatter | solution.py:255
  1503.1 611.6 %all-reduce.11.cloned.1.call-start = ((), (), s32[]{:S(2)}) async-start(), calls=%async_computation.11 | async-start | bytes 58720256 | tf_op jit(solution)/shard_map/psum | solution.py:269
  1503.2 36.1 %slice-start = ((s8[9437184]{0:T(1024)(128)(4,1)}), s8[4194304]{0:T(1024)(128)(4,1)S(1)}, s32[]{:S(2)}) async-start(s8[9437184]{0:T(1024)(128)(4,1)} %bitcast.166), calls=%async_computation.12 | async-start | bytes 8388608
  1503.2 36.1 %slice-start.1 = ((s8[9437184]{0:T(1024)(128)(4,1)}), s8[4194304]{0:T(1024)(128)(4,1)S(1)}, s32[]{:S(2)}) async-start(s8[9437184]{0:T(1024)(128)(4,1)} %bitcast.166), calls=%async_computation.13 | async-start | bytes 8388608
  1579.7 664.4 %all-reduce.9.cloned.1.call-start = ((), (), s32[]{:S(2)}) async-start(), calls=%async_computation.10 | async-start | bytes 262144 | tf_op jit(solution)/shard_map/psum | solution.py:277
  (79 other events, 435.2 us)
Sparse Core Ops, SparseCore 0:
  12.7 84.7 all-gather.3
  166.1 166.8 reduce-scatter.2
  1363.0 80.8 all-gather.5
  1503.2 88.1 reduce-scatter.4
  1597.1 517.5 all-reduce.10
  2121.6 122.3 all-reduce.8
where the time goes:
time: 2260 us; the launch traced here: 2250 us
  waiting for transfers between devices  1580 us (70%)
  matrix products  264 us (12%)
  local copies, waits for them, and re-layouts  191 us (8%)
  other arithmetic  124 us (5%)
  blocking collectives  52.2 us (2%)
    psum x1, waiting for transfers between devices, local(): lax.psum(grad_query_w.astype(jnp.bfloat16), 'rep').astype(jnp.float32)  478 us
    all_to_all x1, waiting for transfers between devices, local(): lax.all_to_all(send_rows.reshape(expert_count, CAP, model_width), 'shard'...  197 us
    all_to_all x1, waiting for transfers between devices, local(): lax.all_to_all(grad_send.reshape(expert_count, CAP, model_width), 'shard'...  189 us
    all_to_all x1, waiting for transfers between devices, local(): lax.all_to_all(grad_expert_in, 'shard', split_axis=1, concat_axis=0, tile...  163 us
    reduce_scatter x1, waiting for transfers between devices, local(): lax.psum_scatter(jnp.dot(flat_attended, proj_out, preferred_element_type=...  159 us
    all_to_all x1, waiting for transfers between devices, local(): lax.all_to_all(expert_out, 'shard', split_axis=1, concat_axis=0, tiled=True)  152 us
    psum x1, waiting for transfers between devices, local(): lax.psum((grad_gain_attn, grad_gain_query, grad_gain_key, grad_gain_moe,...  85.6 us
    all_gather x1, waiting for transfers between devices, local(): branch_rows = lax.all_gather(grad_branch, 'shard', axis=0, tiled=True)  80.9 us
  transfers between devices with their start and end apart: 10, of which 10 were waited for; matrix products, arithmetic and copies ran while one was open for 12% of the time, Pallas kernels for 0%

commit v1 on v0

--- a/solution.py
+++ b/solution.py
@@ -274,10 +274,9 @@
         lax.psum(grad_up_w.astype(jnp.bfloat16), "rep").astype(jnp.float32),
         lax.psum(grad_down.astype(jnp.bfloat16), "rep").astype(jnp.float32),
     )
-    shared = lax.psum(
-        (grad_gain_attn, grad_gain_query, grad_gain_key, grad_gain_moe, grad_router),
-        ("rep", "shard"),
-    )
+    shared = (grad_gain_attn, grad_gain_query, grad_gain_key, grad_gain_moe, grad_router)
+    for over in ("shard", "rep"):
+        shared = lax.psum(shared, over)
     return (
         output,
         grad_input,

time: 2260 us -> 2170 us (0.960)
  waiting for transfers between devices: 1580 us -> 1490 us
    psum x1 -> x2, waiting for transfers between devices: 85.6 us -> 1.25 us  [local(): shared = lax.psum(shared, over)]
  transfers between devices with their start and end apart: 10 -> 11, of which waited for: 10 -> 10; matrix products, arithmetic and copies ran while one was open for 12% -> 15% of each run, Pallas kernels for 0% -> 0%
where the time goes in v1:
time: 2170 us
  waiting for transfers between devices  1490 us (69%)
  matrix products  265 us (12%)
  local copies, waits for them, and re-layouts  190 us (9%)
  other arithmetic  125 us (6%)
  blocking collectives  57.4 us (3%)
    psum x1, waiting for transfers between devices, local(): lax.psum(grad_query_w.astype(jnp.bfloat16), 'rep').astype(jnp.float32)  474 us
    all_to_all x1, waiting for transfers between devices, local(): lax.all_to_all(send_rows.reshape(expert_count, CAP, model_width), 'shard'...  197 us
    all_to_all x1, waiting for transfers between devices, local(): lax.all_to_all(grad_send.reshape(expert_count, CAP, model_width), 'shard'...  189 us
    all_to_all x1, waiting for transfers between devices, local(): lax.all_to_all(grad_expert_in, 'shard', split_axis=1, concat_axis=0, tile...  163 us
    reduce_scatter x1, waiting for transfers between devices, local(): lax.psum_scatter(jnp.dot(flat_attended, proj_out, preferred_element_type=...  159 us
    all_to_all x1, waiting for transfers between devices, local(): lax.all_to_all(expert_out, 'shard', split_axis=1, concat_axis=0, tiled=True)  152 us
    all_gather x1, waiting for transfers between devices, local(): branch_rows = lax.all_gather(grad_branch, 'shard', axis=0, tiled=True)  78.5 us
    all_gather x1, waiting for transfers between devices, local(): lax.all_gather(normed_low, 'shard', axis=0, tiled=True)  69.1 us
  transfers between devices with their start and end apart: 11, of which 10 were waited for; matrix products, arithmetic and copies ran while one was open for 15% of the time, Pallas kernels for 0%

profile of v1, /device:TPU:0, one launch (start us, length us, event | category | flops | bytes accessed | tf_op | source)
XLA Modules:
  0.0 2168.9 jit_solution(2945911509643692916)
XLA Ops:
  28.4 69.1 %all-gather.4.cloned.1.call-done = bf16[2048,2048]{1,0:T(8,128)(2,1)} async-done(((bf16[256,2048]{1,0:T(8,128)(2,1)}), bf16[2048,2048]{1,0:T(8,128)(2,1)}) %all-gather.4.cloned.1.call-update) | async-done | bytes 8388624 | tf_op jit(solution)/shard_map/all_gather | solution.py:124
  174.2 158.8 %reduce-scatter.3.cloned.1.call-done = f32[256,2048]{1,0:T(8,128)} async-done(((f32[2048,2048]{1,0:T(8,128)}), f32[256,2048]{1,0:T(8,128)}) %reduce-scatter.3.cloned.1.call-update) | async-done | bytes 2097168 | tf_op jit(solution)/shard_map/reduce_scatter | solution.py:140
  339.4 18.5 scatter_custom_fusion.1
  363.4 17.6 scatter_custom_fusion
  381.0 188.8 %all-to-all-done.2 = bf16[16,144,2048]{2,1,0:T(8,128)(2,1)} async-done(((bf16[16,144,2048]{2,1,0:T(8,128)(2,1)}), bf16[16,144,2048]{2,1,0:T(8,128)(2,1)}, u32[]{:S(2)}, u32[]{:S(2)}) %all-to-all-start.2) | async-done | bytes 9437216 | tf_op jit(solution)/shard_map/all_to_all | solution.py:185
  584.3 197.1 %all-to-all-done = bf16[16,144,2048]{2,1,0:T(8,128)(2,1)} async-done(((bf16[16,144,2048]{2,1,0:T(8,128)(2,1)}), bf16[16,144,2048]{2,1,0:T(8,128)(2,1)}, u32[]{:S(2)}, u32[]{:S(2)}) %all-to-all-start) | async-done | bytes 9437216 | tf_op jit(solution)/shard_map/all_to_all | solution.py:156
  790.8 17.2 fusion.76
  822.5 23.1 %multiply_convert_fusion = (bf16[2,1152,1024]{2,1,0:T(8,128)(2,1)}, bf16[2,1152,1024]{2,1,0:T(8,128)(2,1)}, bf16[2,1152,1024]{2,1,0:T(8,128)(2,1)}) fusion(f32[2,1152,1024]{2,1,0:T(8,128)} %fusion.75, f32[2,1152,1024]{2,1,0:T(8,128)} %fusion.76, bf16[2,1152,2048]{2,1,0:T(8,128)(2,1)} %bitcast.161, bf16[2,1024,2048]{2,1,0:T(8,128)(2,1)} %param.30), kind=kOutput, calls=%fused_computation.14 | convolution fusion | flops 9699065856 | bytes 50855936 | tf_op jit(solution)/shard_map/erd,efd->erf/dot_general | solution.py:192
  859.9 27.9 %copy.302 = bf16[2,1152,2048]{2,0,1:T(2,128)(2,1)} copy(bf16[2,1152,2048]{2,1,0:T(8,128)(2,1)S(1)} %convolution_convert_fusion) | data formatting | bytes 18874368 | tf_op jit(solution)/shard_map/convert_element_type | solution.py:170
  893.1 17.5 fusion.77
  910.5 18.6 add_convert_fusion
  929.2 18.2 copy.307
  947.4 152.1 %all-to-all-done.1 = bf16[2,1152,2048]{2,0,1:T(2,128)(2,1)} async-done(((bf16[2,1152,2048]{2,0,1:T(2,128)(2,1)}), bf16[2,1152,2048]{2,0,1:T(2,128)(2,1)}, u32[]{:S(2)}, u32[]{:S(2)}) %all-to-all-start.1) | async-done | bytes 9437216 | tf_op jit(solution)/shard_map/all_to_all | solution.py:171
  1116.6 21.8 %gather_fusion = bf16[2048,2048]{1,0:T(8,128)(2,1)} fusion(bf16[2304,2048]{1,0:T(8,128)(2,1)} %bitcast.158, s32[2048]{0:T(1024)S(1)} %broadcast_clamp_fusion), kind=kCustom, calls=%fused_computation | custom fusion | bytes 16785408 | tf_op jit(solution)/shard_map/gather | solution.py:174
  1148.1 162.8 %all-to-all-done.3 = bf16[2,1152,2048]{2,0,1:T(2,128)(2,1)} async-done(((bf16[2,1152,2048]{2,0,1:T(2,128)(2,1)}), bf16[2,1152,2048]{2,0,1:T(2,128)(2,1)}, u32[]{:S(2)}, u32[]{:S(2)}) %all-to-all-start.3) | async-done | bytes 9437216 | tf_op jit(solution)/shard_map/all_to_all | solution.py:208
  1322.7 21.4 gather_fusion.1
  1365.1 78.5 %all-gather.6.cloned.1.call-done = bf16[2048,2048]{1,0:T(8,128)(2,1)} async-done(((bf16[256,2048]{1,0:T(8,128)(2,1)}), bf16[2048,2048]{1,0:T(8,128)(2,1)}) %all-gather.6.cloned.1.call-update) | async-done | bytes 8388624 | tf_op jit(solution)/shard_map/all_gather | solution.py:227
  1487.5 15.7 add_convert_fusion.1
  1503.2 18.2 convolution_convert_fusion.1
  1521.5 17.2 convolution_convert_fusion.2
  1538.7 15.7 convolution_convert_fusion.3
  1597.5 25.9 %all-reduce.4 = (f32[2048]{0:T(1024)S(1)}, f32[128]{0:T(128)S(1)}, f32[128]{0:T(128)S(1)}, f32[2048]{0:T(1024)S(1)}) all-reduce(f32[2048]{0:T(1024)S(1)} %get-tuple-element.22, f32[128]{0:T(128)S(1)} %get-tuple-element.60, f32[128]{0:T(128)S(1)} %get-tuple-element.18, ...), channel_id=1, replica_groups=mesh['rep'=4,'shard'=8] {'shard'}, use_global_device_ids=true, to_apply=%region_27.28 | all-reduce | flops 4352 | bytes 34816 | tf_op jit(solution)/shard_map/psum | solution.py:279
  1623.5 18.0 all-reduce.5
  1641.5 473.9 %all-reduce.15.cloned.1.call-done = (bf16[2048,256]{1,0:T(8,128)(2,1)}, bf16[2048,256]{1,0:T(8,128)(2,1)}, bf16[2048,256]{1,0:T(8,128)(2,1)}, bf16[256,2048]{1,0...) async-done(((bf16[2048,256]{1,0:T(8,128)(2,1)}, bf16[2048,256]{1,0:T(8,128)(2,1)}, ...) | async-done | bytes 29360144 | tf_op jit(solution)/shard_map/psum | solution.py:269
  (315 shorter events, 359.2 us)
Async XLA Ops:
  7.2 150.2 %copy-start = (bf16[256,2048]{1,0:T(8,128)(2,1)S(1)}, bf16[256,2048]{1,0:T(8,128)(2,1)}, u32[]{:S(2)}) copy-start(bf16[256,2048]{1,0:T(8,128)(2,1)} %param.25) | copy-start | bytes 3145732
  7.2 90.3 %copy-start.32 = (bf16[2048,256]{1,0:T(8,128)(2,1)S(1)}, bf16[2048,256]{1,0:T(8,128)(2,1)}, u32[]{:S(2)}) copy-start(bf16[2048,256]{1,0:T(8,128)(2,1)} %param.23) | copy-start | bytes 3145732
  7.2 90.3 %all-gather.4.cloned.1.call-start = ((), (), s32[]{:S(2)}) async-start(), calls=%async_computation.6 | async-start | bytes 9437184 | tf_op jit(solution)/shard_map/all_gather | solution.py:124
  12.6 320.4 %reduce-scatter.3.cloned.1.call-start = ((), (), s32[]{:S(2)}) async-start(), calls=%async_computation.7 | async-start | bytes 18874368 | tf_op jit(solution)/shard_map/reduce_scatter | solution.py:140
  114.4 33.7 %copy-start.3 = (f32[8,256,2,128]{1,3,2,0:T(8,128)}, f32[8,256,2,128]{1,3,2,0:T(8,128)S(1)}, u32[]{:S(2)}) copy-start(f32[8,256,2,128]{1,3,2,0:T(8,128)S(1)} %copy.292) | copy-start | bytes 6291460
  166.7 166.3 %copy-start.8 = (bf16[256,2048]{1,0:T(8,128)(2,1)S(1)}, bf16[256,2048]{1,0:T(8,128)(2,1)}, u32[]{:S(2)}) copy-start(bf16[256,2048]{1,0:T(8,128)(2,1)} %param.16) | copy-start | bytes 3145732
  172.4 162.5 %copy-start.80 = (f32[256]{0:T(256)}, f32[256]{0:T(256)S(1)}, u32[]{:S(2)}) copy-start(f32[256]{0:T(256)S(1)} %compare_convert_fusion) | copy-start | bytes 3076
  172.7 190.7 %copy-start.62 = (s32[2048,1]{0,1:T(1,128)}, s32[2048,1]{0,1:T(1,128)S(1)}, u32[]{:S(2)}) copy-start(s32[2048,1]{0,1:T(1,128)S(1)} %compare_select_fusion) | copy-start | bytes 24580
  172.7 163.6 %copy-start.57 = (f32[2048]{0:T(1024)S(1)}, f32[2048]{0:T(1024)}, u32[]{:S(2)}) copy-start(f32[2048]{0:T(1024)} %param.26) | copy-start | bytes 24580
  174.2 163.3 %copy-start.38 = (bf16[2048,16]{0,1:T(8,128)(2,1)S(1)}, bf16[2048,16]{0,1:T(8,128)(2,1)}, u32[]{:S(2)}) copy-start(bf16[2048,16]{0,1:T(8,128)(2,1)} %param.27) | copy-start | bytes 196612
  358.0 211.7 %all-to-all-start.2 = ((bf16[16,144,2048]{2,1,0:T(8,128)(2,1)}), bf16[16,144,2048]{2,1,0:T(8,128)(2,1)}, u32[]{:S(2)}, u32[]{:S(2)}) async-start(bf16[16,144,2048]{2,1,0:T(8,128)(2,1)} %bitcast.160), calls=%async_computation.3 | async-start | bytes 18874368 | tf_op jit(solution)/shard_map/all_to_all | solution.py:185
  569.7 211.7 %all-to-all-start = ((bf16[16,144,2048]{2,1,0:T(8,128)(2,1)}), bf16[16,144,2048]{2,1,0:T(8,128)(2,1)}, u32[]{:S(2)}, u32[]{:S(2)}) async-start(bf16[16,144,2048]{2,1,0:T(8,128)(2,1)} %bitcast.159), calls=%async_computation.1 | async-start | bytes 18874368 | tf_op jit(solution)/shard_map/all_to_all | solution.py:156
  887.8 211.6 %all-to-all-start.1 = ((bf16[2,1152,2048]{2,0,1:T(2,128)(2,1)}), bf16[2,1152,2048]{2,0,1:T(2,128)(2,1)}, u32[]{:S(2)}, u32[]{:S(2)}) async-start(bf16[2,1152,2048]{2,0,1:T(2,128)(2,1)} %copy.302), calls=%async_computation.2 | async-start | bytes 18874368 | tf_op jit(solution)/shard_map/all_to_all | solution.py:171
  947.4 157.4 %copy-start.63 = (s32[2048,1]{0,1:T(1,128)S(1)}, s32[2048,1]{0,1:T(1,128)}, u32[]{:S(2)}) copy-start(s32[2048,1]{0,1:T(1,128)} %copy-done.62) | copy-start | bytes 24580
  1099.4 211.4 %all-to-all-start.3 = ((bf16[2,1152,2048]{2,0,1:T(2,128)(2,1)}), bf16[2,1152,2048]{2,0,1:T(2,128)(2,1)}, u32[]{:S(2)}, u32[]{:S(2)}) async-start(bf16[2,1152,2048]{2,0,1:T(2,128)(2,1)} %copy.307), calls=%async_computation.4 | async-start | bytes 18874368 | tf_op jit(solution)/shard_map/all_to_all | solution.py:208
  1104.5 339.0 %all-gather.6.cloned.1.call-start = ((), (), s32[]{:S(2)}) async-start(), calls=%async_computation.8 | async-start | bytes 9437184 | tf_op jit(solution)/shard_map/all_gather | solution.py:227
  1116.6 21.8 %copy-start.11 = (f32[256,2048]{1,0:T(8,128)S(1)}, f32[256,2048]{1,0:T(8,128)}, u32[]{:S(2)}) copy-start(f32[256,2048]{1,0:T(8,128)} %convert_multiply_fusion.8) | copy-start | bytes 6291460
  1116.6 21.8 %copy-start.30 = (f32[256,8]{1,0:T(8,128)S(1)}, f32[256,8]{1,0:T(8,128)}, u32[]{:S(2)}) copy-start(f32[256,8]{1,0:T(8,128)} %copy-done.29) | copy-start | bytes 24580
  1362.5 216.6 %all-reduce.11.cloned.1.call-start = ((), (), s32[]{:S(2)}) async-start(), calls=%async_computation.10 | async-start | bytes 262144 | tf_op jit(solution)/shard_map/psum | solution.py:279
  1365.0 226.4 %reduce-scatter.5.cloned.1.call-start = ((), (), s32[]{:S(2)}) async-start(), calls=%async_computation.9 | async-start | bytes 9437184 | tf_op jit(solution)/shard_map/reduce_scatter | solution.py:255
  1503.2 612.2 %all-reduce.15.cloned.1.call-start = ((), (), s32[]{:S(2)}) async-start(), calls=%async_computation.12 | async-start | bytes 58720256 | tf_op jit(solution)/shard_map/psum | solution.py:269
  1503.2 35.5 %slice-start = ((s8[9437184]{0:T(1024)(128)(4,1)}), s8[4194304]{0:T(1024)(128)(4,1)S(1)}, s32[]{:S(2)}) async-start(s8[9437184]{0:T(1024)(128)(4,1)} %bitcast.166), calls=%async_computation.13 | async-start | bytes 8388608
  1503.2 35.5 %slice-start.1 = ((s8[9437184]{0:T(1024)(128)(4,1)}), s8[4194304]{0:T(1024)(128)(4,1)S(1)}, s32[]{:S(2)}) async-start(s8[9437184]{0:T(1024)(128)(4,1)} %bitcast.166), calls=%async_computation.14 | async-start | bytes 8388608
  1579.0 581.2 %all-reduce.13.cloned.1.call-start = ((), (), s32[]{:S(2)}) async-start(), calls=%async_computation.11 | async-start | bytes 262144 | tf_op jit(solution)/shard_map/psum | solution.py:279
  (74 other events, 414.0 us)
Sparse Core Ops, SparseCore 0:
  12.7 84.7 all-gather.3
  166.1 166.8 reduce-scatter.2
  1362.6 80.8 all-gather.5
  1445.7 52.7 all-reduce.10
  1503.3 88.1 reduce-scatter.4
  1597.9 517.4 all-reduce.14
  2118.2 41.9 all-reduce.12
